TPU v7x, 512 devices: a whole 4x8x8 slice. The times are simulated.
512 devices in a mesh: dp: 16 (over z, core), expert: 32 (over y, x).
Axes of the slice: x: 4, y: 8, z: 8, core: 2. Of those that a mesh axis runs over, the one named last changes fastest.
Arguments:
- tokens: bfloat16 [2048, 4096], P(('dp', 'expert')), may hold values from -6 to 6
- expert_ids: int32 [2048, 8], P(('dp', 'expert')), may hold values from 0 to 31, all different within a row; in each aligned block of 4 rows (0 to 3, 4 to 7, ...) at most 2 rows name the same one
- gate_probs: float32 [2048, 8], P(('dp', 'expert')), may hold values from 0.2 to 1
- w_gate: bfloat16 [32, 4096, 2048], P('expert', None, 'dp'), may hold values from -0.09375 to 0.09375
- w_up: bfloat16 [32, 4096, 2048], P('expert', None, 'dp'), may hold values from -0.09375 to 0.09375
- w_down: bfloat16 [32, 2048, 4096], P('expert', None, 'dp'), may hold values from -0.125 to 0.125
Outputs:
- combined: bfloat16 [2048, 4096], P(('dp', 'expert'))
Inputs may be any that keep to these rules, and one draw needn't show every extreme that they name: `expert_ids`: each row names 8 different experts. In the rows of one device (aligned blocks of 4 rows) no expert is named by more than 2 rows, a bound that some block reaches.
All inputs are finite; a program needn't handle non-finite values.
Results may differ from a plain program's by a relative error of at most 0.0057.
Values may be sent and summed in bfloat16 or wider, within the bound.
A program may use at most 64 MiB of HBM per device.

v0:
```python
import jax
import jax.numpy as jnp
from jax import lax
from jax.sharding import PartitionSpec as P


def slot_positions(choices, experts, capacity):
    flat_ids = choices.reshape(-1)
    onehot = (flat_ids[:, None] == jnp.arange(experts, dtype=jnp.int32)[None, :]).astype(jnp.int32)
    earlier = jnp.cumsum(onehot, axis=0) - onehot
    slot_rank = jnp.sum(earlier * onehot, axis=1)
    return flat_ids * capacity + slot_rank


def placement_table(choices, experts, capacity):
    token_count, top_count = choices.shape
    positions = slot_positions(choices, experts, capacity)
    chosen = (
        positions[:, None] == jnp.arange(experts * capacity, dtype=jnp.int32)[None, :]
    ).astype(jnp.float32)
    return chosen.reshape(token_count, top_count, experts * capacity)


def local(tokens, expert_ids, gate_probs, w_gate, w_up, w_down):
    token_count, width = tokens.shape
    top_count = expert_ids.shape[1]
    groups = lax.axis_size("dp")
    experts = lax.axis_size("expert") * w_gate.shape[0]
    capacity = min(token_count, max(2, 2 * token_count * top_count // experts))
    gate_matrix = w_gate[0]
    up_matrix = w_up[0]
    down_matrix = w_down[0]
    chosen = placement_table(expert_ids, experts, capacity)
    placing = jnp.sum(chosen, axis=1).astype(jnp.bfloat16)
    outgoing = jnp.einsum("tp,td->pd", placing, tokens, preferred_element_type=jnp.float32)
    outgoing = outgoing.astype(jnp.bfloat16).reshape(experts, capacity, width)
    arrived = lax.all_to_all(outgoing, "expert", split_axis=0, concat_axis=0, tiled=True)
    row_block = lax.all_gather(arrived.reshape(experts * capacity, width), "dp", axis=0, tiled=True)
    gate_proj = jnp.dot(row_block, gate_matrix, preferred_element_type=jnp.float32)
    up_proj = jnp.dot(row_block, up_matrix, preferred_element_type=jnp.float32)
    hidden = (jax.nn.silu(gate_proj) * up_proj).astype(jnp.bfloat16)
    columns = jnp.dot(
        lax.all_gather(hidden, "dp", axis=1, tiled=True),
        down_matrix,
        preferred_element_type=jnp.float32,
    ).astype(jnp.bfloat16)
    out_blocks = columns.reshape(groups, experts, capacity, down_matrix.shape[1])
    returned = lax.all_to_all(
        lax.all_to_all(out_blocks, "dp", split_axis=0, concat_axis=3, tiled=True),
        "expert",
        split_axis=1,
        concat_axis=1,
        tiled=True,
    )
    returned = returned.reshape(experts * capacity, width).astype(jnp.float32)
    weighting = jnp.einsum("tkp,tk->tp", chosen, gate_probs, precision=lax.Precision.HIGHEST)
    combined = jnp.dot(weighting, returned, precision=lax.Precision.HIGHEST)
    return combined.astype(jnp.bfloat16)


def solution(mesh):
    placed = (
        P(("dp", "expert"), None),
        P(("dp", "expert"), None),
        P(("dp", "expert"), None),
        P("expert", None, "dp"),
        P("expert", None, "dp"),
        P("expert", None, "dp"),
    )
    return jax.shard_map(
        local, mesh=mesh, in_specs=placed, out_specs=P(("dp", "expert"), None), check_vma=False
    )
```

profile of v0, /device:TPU:1, one launch (start us, length us, event | category | flops | bytes accessed | tf_op | source)
XLA Modules:
  0.0 219.0 jit_solution(1981563794429632144)
XLA Ops:
  6.5 0.0 copy-start
  6.5 0.0 all-gather.3.cloned.1.call-start
  6.5 0.9 eq.30
  7.5 0.1 fusion.6
  7.5 0.1 reduce_window_sum.11
  7.6 0.2 select_reduce_fusion
  7.8 0.1 reduce_sum.21
  7.9 0.7 multiply_add_fusion
  8.5 0.1 convert_reduce_fusion
  8.6 1.1 convolution_convert_fusion
  9.7 0.3 reshape.39
  10.1 26.6 %all_to_all.28 = bf16[32,2,4096]{2,1,0:T(2,128)(2,1)S(1)} all-to-all(bf16[32,2,4096]{2,1,0:T(2,128)(2,1)S(1)} %reshape.39), channel_id=1, replica_groups=mesh['dp'=16,'expert'=32] {'expert'}, dimensions={0} | all-to-all | bytes 1048576 | tf_op jit(solution)/shard_map/all_to_all | solution.py:37
  36.7 1.0 reshape.40
  37.7 0.0 all-gather.3.cloned.1.call-update
  37.7 0.0 all-gather.5.cloned.1.call-start
  37.8 60.9 %all-gather.3.cloned.1.call-done = bf16[1024,4096]{1,0:T(8,128)(2,1)} async-done(((bf16[64,4096]{1,0:T(8,128)(2,1)}), bf16[1024,4096]{1,0:T(8,128)(2,1)}) %all-gather.3.cloned.1.call-update) | async-done | bytes 8388624 | tf_op jit(solution)/shard_map/all_gather | solution.py:38
  98.7 6.1 %fusion.3 = f32[1024,128]{1,0:T(8,128)S(1)} fusion(bf16[1024,4096]{1,0:T(8,128)(2,1)} %all-gather.3.cloned.1.call-done, bf16[1,4096,128]{2,1,0:T(8,128)(2,1)} %param.9), kind=kOutput, calls=%fused_computation.7 | convolution fusion | flops 1073741824 | bytes 9961472 | tf_op jit(solution)/shard_map/dot_general | solution.py:39
  104.7 0.0 copy-done.2
  104.8 3.0 %fusion = bf16[1024,128]{1,0:T(8,128)(2,1)} fusion(bf16[1024,4096]{1,0:T(8,128)(2,1)S(1)} %copy-done.1, bf16[1,4096,128]{2,1,0:T(8,128)(2,1)S(1)} %copy-done.2, f32[1024,128]{1,0:T(8,128)S(1)} %fusion.3), kind=kOutput, calls=%fused_computation.4 | convolution fusion | flops 1074528256 | bytes 10223616 | tf_op jit(solution)/shard_map/dot_general | solution.py:40
  107.8 0.0 all-gather.5.cloned.1.call-update
  107.8 50.9 %all-gather.5.cloned.1.call-done = bf16[1024,2048]{1,0:T(8,128)(2,1)} async-done(((bf16[1024,128]{1,0:T(8,128)(2,1)}), bf16[1024,2048]{1,0:T(8,128)(2,1)}) %all-gather.5.cloned.1.call-update) | async-done | bytes 4194320 | tf_op jit(solution)/shard_map/all_gather | solution.py:43
  158.7 3.4 %convolution_convert_fusion.2 = bf16[1024,256]{1,0:T(8,128)(2,1)S(1)} fusion(bf16[1024,2048]{1,0:T(8,128)(2,1)} %all-gather.5.cloned.1.call-done, bf16[1,2048,256]{2,1,0:T(8,128)(2,1)S(1)} %copy-done), kind=kOutput, calls=%fused_computation.2 | convolution fusion | flops 1074003968 | bytes 5767168 | tf_op jit(solution)/shard_map/dot_general | solution.py:42
  162.1 0.2 reshape.41
  162.3 0.1 copy.13
  162.4 21.2 %all_to_all.29 = bf16[16,32,2,256]{3,1,2,0:T(8,128)(2,1)S(1)} all-to-all(bf16[16,32,2,256]{3,1,2,0:T(8,128)(2,1)S(1)} %copy.13), channel_id=1, replica_groups=mesh['dp'=16,'expert'=32] {'dp'}, dimensions={0} | all-to-all | bytes 1048576 | tf_op jit(solution)/shard_map/all_to_all | solution.py:49
  183.7 0.3 copy.18
  184.0 0.9 reshape.45
  184.9 9.1 %all-to-all-start.2 = ((bf16[1,32,2,4096]{3,2,0,1:T(2,128)(2,1)}), bf16[1,32,2,4096]{3,2,0,1:T(2,128)(2,1)S(1)}, u32[]{:S(2)}, u32[]{:S(2)}) async-start(bf16[1,32,2,4096]{3,2,0,1:T(2,128)(2,1)} %reshape.45), calls=%async_computation.2 | async-start | bytes 1048576 | tf_op jit(solution)/shard_map/all_to_all | solution.py:48
  194.0 0.2 fusion.5
  194.2 16.8 %all-to-all-done.2 = bf16[1,32,2,4096]{3,2,0,1:T(2,128)(2,1)S(1)} async-done(((bf16[1,32,2,4096]{3,2,0,1:T(2,128)(2,1)}), bf16[1,32,2,4096]{3,2,0,1:T(2,128)(2,1)S(1)}, u32[]{:S(2)}, u32[]{:S(2)}) %all-to-all-start.2) | async-done | bytes 524320 | tf_op jit(solution)/shard_map/all_to_all | solution.py:48
  211.0 0.2 reshape.42
  211.2 0.9 convolution_convert_fusion.1
  (6 shorter events, 0.0 us)
Async XLA Ops:
  6.5 152.2 %copy-start = (bf16[1,2048,256]{2,1,0:T(8,128)(2,1)S(1)}, bf16[1,2048,256]{2,1,0:T(8,128)(2,1)}, u32[]{:S(2)}) copy-start(bf16[1,2048,256]{2,1,0:T(8,128)(2,1)} %param.11) | copy-start | bytes 3145732
  6.5 98.2 %copy-start.2 = (bf16[1,4096,128]{2,1,0:T(8,128)(2,1)S(1)}, bf16[1,4096,128]{2,1,0:T(8,128)(2,1)}, u32[]{:S(2)}) copy-start(bf16[1,4096,128]{2,1,0:T(8,128)(2,1)} %param.10) | copy-start | bytes 3145732
  6.5 92.1 %all-gather.3.cloned.1.call-start = ((), (), s32[]{:S(2)}) async-start(), calls=%async_computation.3 | async-start | bytes 8912896 | tf_op jit(solution)/shard_map/all_gather | solution.py:38
  37.7 121.0 %all-gather.5.cloned.1.call-start = ((), (), s32[]{:S(2)}) async-start(), calls=%async_computation.4 | async-start | bytes 4456448 | tf_op jit(solution)/shard_map/all_gather | solution.py:43
  98.7 6.1 %copy-start.1 = (bf16[1024,4096]{1,0:T(8,128)(2,1)S(1)}, bf16[1024,4096]{1,0:T(8,128)(2,1)}, u32[]{:S(2)}) copy-start(bf16[1024,4096]{1,0:T(8,128)(2,1)} %all-gather.3.cloned.1.call-done) | copy-start | bytes 25165828
  107.8 86.2 %copy-start.3 = (f32[4,8]{1,0:T(4,128)S(1)}, f32[4,8]{1,0:T(4,128)}, u32[]{:S(2)}) copy-start(f32[4,8]{1,0:T(4,128)} %param.8) | copy-start | bytes 388
  184.9 26.1 %all-to-all-start.2 = ((bf16[1,32,2,4096]{3,2,0,1:T(2,128)(2,1)}), bf16[1,32,2,4096]{3,2,0,1:T(2,128)(2,1)S(1)}, u32[]{:S(2)}, u32[]{:S(2)}) async-start(bf16[1,32,2,4096]{3,2,0,1:T(2,128)(2,1)} %reshape.45), calls=%async_computation.2 | async-start | bytes 1048576 | tf_op jit(solution)/shard_map/all_to_all | solution.py:48
Sparse Core Ops, SparseCore 0:
  37.8 60.7 all-gather.2
  107.9 50.6 all-gather.4
where the time goes:
time: 219 us
  waiting for transfers between devices  129 us (59%)
  blocking collectives  47.8 us (22%)
  matrix products  14.8 us (7%)
  between operations  13.5 us (6%)
  starting transfers between devices  9.17 us (4%)
  local copies, waits for them, and re-layouts  4.07 us (2%)
    all_gather x1, waiting for transfers between devices, local(): lax.all_gather(arrived.reshape(experts * capacity, width), 'dp', axis=0,...  60.9 us
    all_gather x1, waiting for transfers between devices, local(): lax.all_gather(hidden, 'dp', axis=1, tiled=True)  50.9 us
    all_to_all x1, blocking collectives, local(): lax.all_to_all(outgoing, 'expert', split_axis=0, concat_axis=0, tiled=True)  26.6 us
    all_to_all x1, blocking collectives, local(): lax.all_to_all(out_blocks, 'dp', split_axis=0, concat_axis=3, tiled=True)  21.2 us
    all_to_all x1, waiting for transfers between devices, local(): lax.all_to_all(lax.all_to_all(out_blocks, 'dp', split_axis=0, concat_axis...  16.8 us
    all_to_all x1, starting transfers between devices, local(): lax.all_to_all(lax.all_to_all(out_blocks, 'dp', split_axis=0, concat_axis...  9.13 us
    dot_general x1, matrix products, local(): jnp.dot(row_block, gate_matrix, preferred_element_type=jnp.float32)  6.08 us
  transfers between devices with their start and end apart: 3, of which 3 were waited for; matrix products, arithmetic and copies ran while one was open for 0% of the time, Pallas kernels for 0%

commit v1 on v0

v1 whole, which is shorter than its diff:
```python
import jax
import jax.numpy as jnp
from jax import lax
from jax.experimental import pallas as pl
from jax.experimental.pallas import tpu as pltpu
from jax.sharding import PartitionSpec as P

MESH = pl.DeviceIdType.MESH
NX, NY, NZ = 4, 8, 8
NE = NX * NY
F32, BF16 = jnp.float32, jnp.bfloat16


def iota(shape, dim):
    return lax.broadcasted_iota(jnp.int32, shape, dim)


def kernel(
    tok_in, meta_in, wg, wu, wd, out,
    tok, metaz, wgu, wdn, xs, hid, outb, rbuf, wrow, fin, final,
    lsem, wssem, wrsem, zssem, zrsem, mssem, mrsem, ssem, rsem,
    hssem, hrsem, ossem, orsem, fssem, frsem,
):
    dp = lax.axis_index("dp")
    ex = lax.axis_index("expert")
    z, core = dp // 2, dp % 2
    y, x = ex // NX, ex % NX
    first = core == 0

    local = [
        pltpu.make_async_copy(wg.at[0], wgu.at[core, :, pl.ds(0, 128)], lsem.at[0]),
        pltpu.make_async_copy(wu.at[0], wgu.at[core, :, pl.ds(128, 128)], lsem.at[1]),
        pltpu.make_async_copy(wd.at[0], wdn.at[core], lsem.at[2]),
        pltpu.make_async_copy(tok_in, tok.at[ex, pl.ds(z * 8, 8)], lsem.at[3]),
        pltpu.make_async_copy(meta_in, metaz.at[z], lsem.at[4]),
    ]
    for copy in local:
        copy.start()

    barrier = pltpu.get_barrier_semaphore()

    def greet(step, carry):
        peer = lax.rem(ex + step, NE)
        pl.semaphore_signal(barrier, inc=1, device_id=(dp, peer), device_id_type=MESH)
        return carry

    lax.fori_loop(1, NE, greet, 0)
    for step in range(1, NZ):
        peer = lax.rem(z + step, NZ) * 2 + core
        pl.semaphore_signal(barrier, inc=1, device_id=(peer, ex), device_id_type=MESH)
    pl.semaphore_signal(barrier, inc=1, device_id=(z * 2 + 1 - core, ex), device_id_type=MESH)
    pl.semaphore_wait(barrier, NE - 1 + NZ - 1 + 1)

    def z_copy(step):
        peer = lax.rem(z + step, NZ)
        return (
            pltpu.make_async_remote_copy(
                meta_in, metaz.at[z], mssem.at[step], mrsem.at[z],
                device_id=(peer * 2 + core, ex), device_id_type=MESH),
            pltpu.make_async_remote_copy(
                tok_in, tok.at[ex, pl.ds(z * 8, 8)], zssem.at[step], zrsem.at[z],
                device_id=(peer * 2 + core, ex), device_id_type=MESH),
        )

    for step in (4, 3, 5, 2, 6, 1, 7):
        for copy in z_copy(step):
            copy.start()

    sibling = (z * 2 + 1 - core, ex)
    weights = [
        pltpu.make_async_remote_copy(
            wg.at[0], wgu.at[core, :, pl.ds(0, 128)], wssem.at[0], wrsem.at[0],
            device_id=sibling, device_id_type=MESH),
        pltpu.make_async_remote_copy(
            wu.at[0], wgu.at[core, :, pl.ds(128, 128)], wssem.at[1], wrsem.at[1],
            device_id=sibling, device_id_type=MESH),
        pltpu.make_async_remote_copy(
            wd.at[0], wdn.at[core], wssem.at[2], wrsem.at[2],
            device_id=sibling, device_id_type=MESH),
    ]
    for copy in weights:
        copy.start()

    local[3].wait()
    local[4].wait()
    for step in range(1, NZ):
        src = lax.rem(z + step, NZ)
        pltpu.make_async_remote_copy(
            meta_in, metaz.at[src], mssem.at[step], mrsem.at[src],
            device_id=sibling, device_id_type=MESH).wait_recv()
    codes = metaz[:, 0, :]
    tok[ex, 64] = jnp.concatenate([codes, jnp.zeros_like(codes)], axis=0).astype(BF16)
    for step in range(1, NZ):
        src = lax.rem(z + step, NZ)
        pltpu.make_async_remote_copy(
            tok_in, tok.at[ex, pl.ds(src * 8, 8)], zssem.at[step], zrsem.at[src],
            device_id=sibling, device_id_type=MESH).wait_recv()

    def place(n, p):
        m = n - 1
        k = m // 2 + 1
        h = m % 2
        i0 = jnp.where(n == 0, p, jnp.where(n == 7, p, 2 * h + p // 2))
        dx0 = jnp.where(i0 == 0, 0, jnp.where(i0 == 1, -1, i0 - 1))
        dy0 = jnp.where(n == 0, 0, jnp.where(n == 7, -4, -k if p % 2 == 0 else k))
        own = (n == 0) | (n == 2)
        opp = n >= 6
        mm = jnp.where(n == 1, 0, n - 2)
        j = jnp.where(own, 2 * n + p, jnp.where(opp, (n - 6) * 4 + p, 2 * mm + p // 2))
        half = (j + 1) // 2
        dy1 = jnp.where(j % 2 == 1, -half, half)
        dx1 = jnp.where(own, 0, jnp.where(opp, 2, -1 if p % 2 == 0 else 1))
        dx = jnp.where(first, dx0, dx1)
        dy = jnp.where(first, dy0, dy1)
        sx = lax.rem(x + dx + NX, NX)
        sy = lax.rem(y + dy + NY, NY)
        mid = (n >= 1) & (n <= 6)
        upto = (k <= 2) | ((k == 3) & (h == (0 if p % 2 == 0 else 1)))
        row = n == 0
        xp0 = row & (p <= 1)
        xm0 = row & (p == 0)
        yp0 = row | (mid & upto & (p % 2 == 0))
        ym0 = row | (mid & upto & (p % 2 == 1))
        side = ~own & ~opp
        xp1 = own | (side & (p == 0))
        xm1 = own | (side & (p == 3))
        yp1 = own & ((j == 0) | ((j % 2 == 1) & (j <= 5)))
        ym1 = own & ((j == 0) | ((j % 2 == 0) & (j >= 2) & (j <= 4)))

        def pick(a, b):
            return (first & a) | (~first & b)

        sends = (pick(xp0, xp1), pick(xm0, xm1), pick(yp0, yp1), pick(ym0, ym1))
        return sy, sx, sends

    right, left = lax.rem(x + 1, NX), lax.rem(x + NX - 1, NX)
    below, above = lax.rem(y + 1, NY), lax.rem(y + NY - 1, NY)
    targets = ((dp, y * NX + right), (dp, y * NX + left), (dp, below * NX + x), (dp, above * NX + x))

    def block_copy(way, idx):
        return pltpu.make_async_remote_copy(
            tok.at[idx], tok.at[idx], ssem.at[way, idx], rsem.at[idx],
            device_id=targets[way], device_id_type=MESH)

    def start_sends(n, p):
        sy, sx, sends = place(n, p)
        idx = sy * NX + sx
        for way in range(4):
            @pl.when(sends[way])
            def _():
                block_copy(way, idx).start()

    def hid_copy(n, step):
        peer = lax.rem(z + step, NZ)
        return pltpu.make_async_remote_copy(
            hid.at[n, z], hid.at[n, z], hssem.at[n, step], hrsem.at[n, z],
            device_id=(peer * 2 + core, ex), device_id_type=MESH)

    def out_copy(n, p):
        sy, sx, _ = place(n, p)
        return pltpu.make_async_remote_copy(
            outb.at[n, p], rbuf.at[ex], ossem.at[n, p], orsem.at[ex],
            device_id=(dp, sy * NX + sx), device_id_type=MESH)

    for way in range(4):
        block_copy(way, ex).start() if way in (2, 3) else None
    for way in (0, 1):
        block_copy(way, ex).start()

    lane = iota((8, 512), 1)
    sub = iota((8, 512), 0)
    depth = iota((128, 512), 0)
    wide = iota((128, 512), 1)
    probs = metaz[:, 1, :]
    hi = probs.astype(BF16)
    rest = probs - hi.astype(F32)
    mid_part = rest.astype(BF16)
    low = (rest - mid_part.astype(F32)).astype(BF16)
    stack = jnp.concatenate([codes.astype(BF16), hi, mid_part, low], axis=0)
    for t in range(4):
        spread = jnp.where(depth == t * 32 + (wide >> 4), 1.0, 0.0).astype(BF16)
        got = jnp.dot(stack, spread, preferred_element_type=F32)
        code = got[0:8]
        prob = got[8:16] + got[16:24] + got[24:32]
        keep = (((lane >> 1) & 7) == sub) & (code == ((lane & 1) + 1).astype(F32))
        wrow[t * 8:(t + 1) * 8, :] = jnp.where(keep, prob, 0.0)

    arow = iota((64, 128), 0)
    rcol = iota((64, 128), 1)
    same = ((rcol & 3) == (arow >> 4)) & ((rcol >> 4) == ((arow >> 1) & 7))
    want = ((arow & 1) + 1).astype(F32)
    zmask = iota((16, 128), 0) == (iota((16, 128), 1) >> 4)
    dl, dr = iota((128, 128), 0), iota((128, 128), 1)
    extract = jnp.where(dl == ((dr >> 2) & 3) * 32 + ex, 1.0, 0.0).astype(BF16)

    def group(n, carry):
        @pl.when(n < 8)
        def _():
            for p in range(4):
                sy, sx, sends = place(n, p)
                idx = sy * NX + sx

                @pl.when((n > 0) | (p > 0))
                def _():
                    block_copy(0, idx).wait_recv()
                    for way in range(4):
                        @pl.when(sends[way])
                        def _():
                            block_copy(way, idx).start()

            @pl.when(n == 0)
            def _():
                for copy in local[:3]:
                    copy.wait()
                for i in range(3):
                    pltpu.make_async_remote_copy(
                        (wg.at[0], wu.at[0], wd.at[0])[i],
                        (wgu.at[1 - core, :, pl.ds(0, 128)], wgu.at[1 - core, :, pl.ds(128, 128)], wdn.at[1 - core])[i],
                        wssem.at[i], wrsem.at[i], device_id=sibling, device_id_type=MESH).wait_recv()

            for p in range(4):
                sy, sx, _ = place(n, p)
                idx = sy * NX + sx
                got = jnp.dot(tok[idx, 64], extract, preferred_element_type=F32)
                crow = jnp.sum(jnp.where(zmask, got, 0.0), axis=0, keepdims=True)
                sel = jnp.where(same & (crow == want), 1.0, 0.0).astype(BF16)
                raw = jnp.concatenate(
                    [jnp.concatenate([tok[idx, zz * 8 + l] for zz in range(NZ)], axis=0) for l in range(8)], axis=1)
                rows = jnp.dot(sel, raw, preferred_element_type=F32).astype(BF16)
                for q in range(4):
                    xs[p * 16:(p + 1) * 16, q * 1024:(q + 1) * 1024] = rows[q * 16:(q + 1) * 16, :]
            data = xs[...]
            for half in range(2):
                both = jnp.dot(data, wgu[half], preferred_element_type=F32)
                g, u = both[:, :128], both[:, 128:]
                hid[n, z, :, half * 128:(half + 1) * 128] = (g / (1.0 + jnp.exp(-g)) * u).astype(BF16)
            for step in (4, 3, 5, 2, 6, 1, 7):
                hid_copy(n, step).start()

        @pl.when(n >= 1)
        def _():
            b = n - 1
            for step in range(1, NZ):
                src = lax.rem(z + step, NZ)
                pltpu.make_async_remote_copy(
                    hid.at[b, src], hid.at[b, src], hssem.at[b, step], hrsem.at[b, src],
                    device_id=sibling, device_id_type=MESH).wait_recv()
            full = jnp.concatenate([hid[b, zz] for zz in range(NZ)], axis=1)
            for half in range(2):
                cols = jnp.dot(full, wdn[half], preferred_element_type=F32).astype(BF16)
                for p in range(4):
                    outb[b, p, :, half * 256:(half + 1) * 256] = cols[p * 16:(p + 1) * 16]
            for p in range(4):
                if p == 0:
                    @pl.when(b > 0)
                    def _():
                        out_copy(b, 0).start()

                    @pl.when(b == 0)
                    def _():
                        rbuf[ex] = outb[0, 0]
                else:
                    out_copy(b, p).start()

        return carry

    lax.fori_loop(0, 9, group, 0)

    def arrived(step, carry):
        src = lax.rem(ex + step, NE)
        pltpu.make_async_remote_copy(
            outb.at[0, 0], rbuf.at[src], ossem.at[0, 0], orsem.at[src],
            device_id=sibling, device_id_type=MESH).wait_recv()
        return carry

    lax.fori_loop(1, NE, arrived, 0)
    w = wrow[...]
    w_hi = w.astype(BF16)
    w_rest = w - w_hi.astype(F32)
    w_mid = w_rest.astype(BF16)
    w_low = (w_rest - w_mid.astype(F32)).astype(BF16)
    three = jnp.dot(
        jnp.concatenate([w_hi, w_mid, w_low], axis=0), rbuf[...].reshape(NE * 16, 512),
        preferred_element_type=F32)
    total = three[0:32] + three[32:64] + three[64:96]
    for t in range(4):
        for zz in range(NZ):
            fin[zz, t:t + 1, :] = total[t * 8 + zz:t * 8 + zz + 1, :]

    def fin_copy(step):
        peer = lax.rem(z + step, NZ)
        return pltpu.make_async_remote_copy(
            fin.at[peer], final.at[z], fssem.at[step], frsem.at[z],
            device_id=(peer * 2 + core, ex), device_id_type=MESH)

    for step in (4, 3, 5, 2, 6, 1, 7):
        fin_copy(step).start()
    final[z] = fin[z]

    for step in range(1, NZ):
        for copy in z_copy(step):
            copy.wait_send()
    for copy in weights:
        copy.wait_send()

    def drained(n, carry):
        for p in range(4):
            sy, sx, sends = place(n, p)
            idx = sy * NX + sx
            for way in range(4):
                @pl.when(sends[way])
                def _():
                    block_copy(way, idx).wait_send()

            @pl.when((n > 0) | (p > 0))
            def _():
                out_copy(n, p).wait_send()
        for step in range(1, NZ):
            hid_copy(n, step).wait_send()
        return carry

    lax.fori_loop(0, 8, drained, 0)
    for step in range(1, NZ):
        src = lax.rem(z + step, NZ)
        pltpu.make_async_remote_copy(
            fin.at[src], final.at[src], fssem.at[step], frsem.at[src],
            device_id=sibling, device_id_type=MESH).wait_recv()
    for zz in range(NZ):
        out[:, zz * 512:(zz + 1) * 512] = final[zz].astype(BF16)
    for step in range(1, NZ):
        fin_copy(step).wait_send()


def local(tokens, expert_ids, gate_probs, w_gate, w_up, w_down):
    count, width = tokens.shape
    named = (expert_ids[:, :, None] == jnp.arange(NE, dtype=jnp.int32)).astype(F32)
    chosen = jnp.sum(named, axis=1)
    before = [jnp.zeros((NE,), F32)]
    for t in range(1, count):
        before.append(before[-1] + chosen[t - 1])
    code = chosen * (1.0 + jnp.stack(before))
    prob = jnp.sum(named * gate_probs[:, :, None], axis=1)
    meta = jnp.concatenate(
        [code.reshape(1, 128), prob.reshape(1, 128), jnp.zeros((6, 128), F32)], axis=0)
    tiles = tokens.reshape(4, 4, 8, 128).transpose(2, 0, 1, 3).reshape(8, 16, 128)
    vmem = pl.BlockSpec(memory_space=pltpu.VMEM)
    hbm = pl.BlockSpec(memory_space=pl.ANY)
    dma = pltpu.SemaphoreType.DMA
    return pl.pallas_call(
        kernel,
        out_shape=jax.ShapeDtypeStruct((count, width), BF16),
        in_specs=[vmem, vmem, hbm, hbm, hbm],
        out_specs=vmem,
        scratch_shapes=[
            pltpu.VMEM((NE, 65, 16, 128), BF16),
            pltpu.VMEM((NZ, 8, 128), F32),
            pltpu.VMEM((2, 4096, 256), BF16),
            pltpu.VMEM((2, 2048, 256), BF16),
            pltpu.VMEM((64, 4096), BF16),
            pltpu.VMEM((8, NZ, 64, 256), BF16),
            pltpu.VMEM((8, 4, 16, 512), BF16),
            pltpu.VMEM((NE, 16, 512), BF16),
            pltpu.VMEM((32, 512), F32),
            pltpu.VMEM((NZ, 4, 512), F32),
            pltpu.VMEM((NZ, 4, 512), F32),
            dma((5,)), dma((3,)), dma((3,)),
            dma((NZ,)), dma((NZ,)), dma((NZ,)), dma((NZ,)),
            dma((4, NE)), dma((NE,)),
            dma((8, NZ)), dma((8, NZ)),
            dma((8, 4)), dma((NE,)),
            dma((NZ,)), dma((NZ,)),
        ],
        compiler_params=pltpu.CompilerParams(collective_id=0, has_side_effects=True),
    )(tiles, meta, w_gate, w_up, w_down)


def solution(mesh):
    placed = (
        P(("dp", "expert"), None),
        P(("dp", "expert"), None),
        P(("dp", "expert"), None),
        P("expert", None, "dp"),
        P("expert", None, "dp"),
        P("expert", None, "dp"),
    )
    return jax.shard_map(
        local, mesh=mesh, in_specs=placed, out_specs=P(("dp", "expert"), None), check_vma=False
    )
```

time: 219 us -> 112 us (0.51)
  the two profiles are of different devices: /device:TPU:1 before, /device:TPU:24 now
where the time goes in v1:
time: 112 us
  Pallas kernels  108 us (96%)
  local copies, waits for them, and re-layouts  2.27 us (2%)
  other arithmetic  1.53 us (1%)
    pallas_call x1, Pallas kernels, local(): pl.pallas_call(kernel, out_shape=jax.ShapeDtypeStruct((count, width), BF1...  108 us

profile of v1, /device:TPU:24, one launch (start us, length us, event | category | flops | bytes accessed | tf_op | source)
XLA Modules:
  0.0 111.7 jit_solution(2050287547039313434)
XLA Ops:
  0.0 0.0 copy-start
  0.0 0.1 pad.2.clone
  0.1 0.8 convert_reduce_fusion
  0.9 0.1 reshape.37
  1.0 0.1 fusion
  1.0 0.1 mul.22
  1.1 0.7 maximum_maximum_fusion.meta_in
  1.8 0.0 copy-done
  1.8 0.6 copy.8
  2.4 107.9 %shard_map.64 = bf16[4,4096]{1,0:T(4,128)(2,1)} custom-call(bf16[8,16,128]{2,1,0:T(8,128)(2,1)} %bitcast.9, f32[8,128]{1,0:T(8,128)} %maximum_maximum_fusion.meta_in, bf16[1,4096,128]{2,1,0:T(8,128)(2,1)} %wg.1, bf16[1,4096,128]{2,1,0:T(8,128)(2,1)} %wu.1, bf16[1,2048,256]{2,1,0:T(8,128)(2,1)} %wd.1), custom_call_target="tpu_custom_call" | custom-call | tf_op jit(solution)/shard_map/pallas_call | solution.py:349
  110.3 1.4 %copy.13 = bf16[4,4096]{1,0:T(4,128)(2,1)} copy(bf16[4,4096]{1,0:T(4,128)(2,1)} %shard_map.64) | data formatting | bytes 65536
  (4 shorter events, 0.0 us)
Async XLA Ops:
  0.0 1.8 %copy-start = (bf16[4,4096]{1,0:T(4,128)(2,1)S(1)}, bf16[4,4096]{1,0:T(4,128)(2,1)}, u32[]{:S(2)}) copy-start(bf16[4,4096]{1,0:T(4,128)(2,1)} %param.6) | copy-start | bytes 98308

commit v2 on v1

--- a/solution.py
+++ b/solution.py
@@ -16,7 +16,8 @@
 
 
 def kernel(
-    tok_in, meta_in, wg, wu, wd, out,
+    tokens, ids, gates, wg, wu, wd, out,
+    tok_in, meta_in,
     tok, metaz, wgu, wdn, xs, hid, outb, rbuf, wrow, fin, final,
     lsem, wssem, wrsem, zssem, zrsem, mssem, mrsem, ssem, rsem,
     hssem, hrsem, ossem, orsem, fssem, frsem,
@@ -31,8 +32,6 @@
         pltpu.make_async_copy(wg.at[0], wgu.at[core, :, pl.ds(0, 128)], lsem.at[0]),
         pltpu.make_async_copy(wu.at[0], wgu.at[core, :, pl.ds(128, 128)], lsem.at[1]),
         pltpu.make_async_copy(wd.at[0], wdn.at[core], lsem.at[2]),
-        pltpu.make_async_copy(tok_in, tok.at[ex, pl.ds(z * 8, 8)], lsem.at[3]),
-        pltpu.make_async_copy(meta_in, metaz.at[z], lsem.at[4]),
     ]
     for copy in local:
         copy.start()
@@ -49,6 +48,25 @@
         peer = lax.rem(z + step, NZ) * 2 + core
         pl.semaphore_signal(barrier, inc=1, device_id=(peer, ex), device_id_type=MESH)
     pl.semaphore_signal(barrier, inc=1, device_id=(z * 2 + 1 - core, ex), device_id_type=MESH)
+
+    at = iota((8, 128), 1)
+    chosen, prob = jnp.zeros((8, 128), F32), jnp.zeros((8, 128), F32)
+    for t in range(4):
+        for k in range(8):
+            hit = at == ids[t:t + 1, k:k + 1] + t * 32
+            chosen = jnp.where(hit, 1.0, chosen)
+            prob = jnp.where(hit, gates[t:t + 1, k:k + 1], prob)
+    before = jnp.zeros((8, 128), F32)
+    for t in range(1, 4):
+        before = before + jnp.where(at >= 32 * t, pltpu.roll(chosen, 32 * t, 1), 0.0)
+    meta_in[...] = jnp.where(iota((8, 128), 0) == 0, chosen * (1.0 + before), prob)
+    metaz[z] = meta_in[...]
+    wide_tokens = tokens[...].astype(F32)
+    for l in range(8):
+        tile = jnp.concatenate(
+            [wide_tokens[:, q * 1024 + l * 128:q * 1024 + (l + 1) * 128] for q in range(4)], axis=0).astype(BF16)
+        tok_in[l] = tile
+        tok[ex, 8 + l] = tile
     pl.semaphore_wait(barrier, NE - 1 + NZ - 1 + 1)
 
     def z_copy(step):
@@ -58,13 +76,18 @@
                 meta_in, metaz.at[z], mssem.at[step], mrsem.at[z],
                 device_id=(peer * 2 + core, ex), device_id_type=MESH),
             pltpu.make_async_remote_copy(
-                tok_in, tok.at[ex, pl.ds(z * 8, 8)], zssem.at[step], zrsem.at[z],
+                tok_in, tok.at[ex, pl.ds((9 - step) % NZ * 8, 8)], zssem.at[step], zrsem.at[NZ - step],
                 device_id=(peer * 2 + core, ex), device_id_type=MESH),
         )
 
-    for step in (4, 3, 5, 2, 6, 1, 7):
-        for copy in z_copy(step):
+    for step in (7, 1, 6, 5, 2, 4, 3):
+        for copy in z_copy(step)[::-1]:
             copy.start()
+
+    def z_arrived(step):
+        pltpu.make_async_remote_copy(
+            tok_in, tok.at[ex, pl.ds((step + 1) % NZ * 8, 8)], zssem.at[step], zrsem.at[step],
+            device_id=sibling, device_id_type=MESH).wait_recv()
 
     sibling = (z * 2 + 1 - core, ex)
     weights = [
@@ -80,21 +103,6 @@
     ]
     for copy in weights:
         copy.start()
-
-    local[3].wait()
-    local[4].wait()
-    for step in range(1, NZ):
-        src = lax.rem(z + step, NZ)
-        pltpu.make_async_remote_copy(
-            meta_in, metaz.at[src], mssem.at[step], mrsem.at[src],
-            device_id=sibling, device_id_type=MESH).wait_recv()
-    codes = metaz[:, 0, :]
-    tok[ex, 64] = jnp.concatenate([codes, jnp.zeros_like(codes)], axis=0).astype(BF16)
-    for step in range(1, NZ):
-        src = lax.rem(z + step, NZ)
-        pltpu.make_async_remote_copy(
-            tok_in, tok.at[ex, pl.ds(src * 8, 8)], zssem.at[step], zrsem.at[src],
-            device_id=sibling, device_id_type=MESH).wait_recv()
 
     def place(n, p):
         m = n - 1
@@ -137,18 +145,11 @@
     below, above = lax.rem(y + 1, NY), lax.rem(y + NY - 1, NY)
     targets = ((dp, y * NX + right), (dp, y * NX + left), (dp, below * NX + x), (dp, above * NX + x))
 
-    def block_copy(way, idx):
+    def block_copy(way, idx, part):
+        piece = tok.at[idx, pl.ds(0, 32)] if part == 0 else tok.at[idx, pl.ds(32, 33)]
         return pltpu.make_async_remote_copy(
-            tok.at[idx], tok.at[idx], ssem.at[way, idx], rsem.at[idx],
+            piece, piece, ssem.at[part, way, idx], rsem.at[part, idx],
             device_id=targets[way], device_id_type=MESH)
-
-    def start_sends(n, p):
-        sy, sx, sends = place(n, p)
-        idx = sy * NX + sx
-        for way in range(4):
-            @pl.when(sends[way])
-            def _():
-                block_copy(way, idx).start()
 
     def hid_copy(n, step):
         peer = lax.rem(z + step, NZ)
@@ -162,10 +163,22 @@
             outb.at[n, p], rbuf.at[ex], ossem.at[n, p], orsem.at[ex],
             device_id=(dp, sy * NX + sx), device_id_type=MESH)
 
-    for way in range(4):
-        block_copy(way, ex).start() if way in (2, 3) else None
-    for way in (0, 1):
-        block_copy(way, ex).start()
+    order = (2, 3, 0, 1)
+    for step in (7, 1, 2):
+        z_arrived(step)
+    for way in order:
+        block_copy(way, ex, 0).start()
+    for step in range(1, NZ):
+        src = lax.rem(z + step, NZ)
+        pltpu.make_async_remote_copy(
+            meta_in, metaz.at[src], mssem.at[step], mrsem.at[src],
+            device_id=sibling, device_id_type=MESH).wait_recv()
+    codes = metaz[:, 0, :]
+    tok[ex, 64] = jnp.concatenate([codes, jnp.zeros_like(codes)], axis=0).astype(BF16)
+    for step in (6, 5, 3, 4):
+        z_arrived(step)
+    for way in order:
+        block_copy(way, ex, 1).start()
 
     lane = iota((8, 512), 1)
     sub = iota((8, 512), 0)
@@ -187,11 +200,12 @@
 
     arow = iota((64, 128), 0)
     rcol = iota((64, 128), 1)
-    same = ((rcol & 3) == (arow >> 4)) & ((rcol >> 4) == ((arow >> 1) & 7))
+    from_z = ((rcol >> 4) + z + 7) & 7
+    same = (((rcol >> 2) & 3) == (arow >> 4)) & (from_z == ((arow >> 1) & 7))
     want = ((arow & 1) + 1).astype(F32)
-    zmask = iota((16, 128), 0) == (iota((16, 128), 1) >> 4)
+    zmask = iota((16, 128), 0) == (((iota((16, 128), 1) >> 4) + z + 7) & 7)
     dl, dr = iota((128, 128), 0), iota((128, 128), 1)
-    extract = jnp.where(dl == ((dr >> 2) & 3) * 32 + ex, 1.0, 0.0).astype(BF16)
+    extract = jnp.where(dl == (dr & 3) * 32 + ex, 1.0, 0.0).astype(BF16)
 
     def group(n, carry):
         @pl.when(n < 8)
@@ -202,15 +216,16 @@
 
                 @pl.when((n > 0) | (p > 0))
                 def _():
-                    block_copy(0, idx).wait_recv()
-                    for way in range(4):
-                        @pl.when(sends[way])
-                        def _():
-                            block_copy(way, idx).start()
+                    for part in range(2):
+                        block_copy(0, idx, part).wait_recv()
+                        for way in range(4):
+                            @pl.when(sends[way])
+                            def _():
+                                block_copy(way, idx, part).start()
 
             @pl.when(n == 0)
             def _():
-                for copy in local[:3]:
+                for copy in local:
                     copy.wait()
                 for i in range(3):
                     pltpu.make_async_remote_copy(
@@ -310,7 +325,8 @@
             for way in range(4):
                 @pl.when(sends[way])
                 def _():
-                    block_copy(way, idx).wait_send()
+                    block_copy(way, idx, 0).wait_send()
+                    block_copy(way, idx, 1).wait_send()
 
             @pl.when((n > 0) | (p > 0))
             def _():
@@ -333,25 +349,17 @@
 
 def local(tokens, expert_ids, gate_probs, w_gate, w_up, w_down):
     count, width = tokens.shape
-    named = (expert_ids[:, :, None] == jnp.arange(NE, dtype=jnp.int32)).astype(F32)
-    chosen = jnp.sum(named, axis=1)
-    before = [jnp.zeros((NE,), F32)]
-    for t in range(1, count):
-        before.append(before[-1] + chosen[t - 1])
-    code = chosen * (1.0 + jnp.stack(before))
-    prob = jnp.sum(named * gate_probs[:, :, None], axis=1)
-    meta = jnp.concatenate(
-        [code.reshape(1, 128), prob.reshape(1, 128), jnp.zeros((6, 128), F32)], axis=0)
-    tiles = tokens.reshape(4, 4, 8, 128).transpose(2, 0, 1, 3).reshape(8, 16, 128)
     vmem = pl.BlockSpec(memory_space=pltpu.VMEM)
     hbm = pl.BlockSpec(memory_space=pl.ANY)
     dma = pltpu.SemaphoreType.DMA
     return pl.pallas_call(
         kernel,
         out_shape=jax.ShapeDtypeStruct((count, width), BF16),
-        in_specs=[vmem, vmem, hbm, hbm, hbm],
+        in_specs=[vmem, vmem, vmem, hbm, hbm, hbm],
         out_specs=vmem,
         scratch_shapes=[
+            pltpu.VMEM((8, 16, 128), BF16),
+            pltpu.VMEM((8, 128), F32),
             pltpu.VMEM((NE, 65, 16, 128), BF16),
             pltpu.VMEM((NZ, 8, 128), F32),
             pltpu.VMEM((2, 4096, 256), BF16),
@@ -363,15 +371,15 @@
             pltpu.VMEM((32, 512), F32),
             pltpu.VMEM((NZ, 4, 512), F32),
             pltpu.VMEM((NZ, 4, 512), F32),
-            dma((5,)), dma((3,)), dma((3,)),
+            dma((3,)), dma((3,)), dma((3,)),
             dma((NZ,)), dma((NZ,)), dma((NZ,)), dma((NZ,)),
-            dma((4, NE)), dma((NE,)),
+            dma((2, 4, NE)), dma((2, NE)),
             dma((8, NZ)), dma((8, NZ)),
             dma((8, 4)), dma((NE,)),
             dma((NZ,)), dma((NZ,)),
         ],
         compiler_params=pltpu.CompilerParams(collective_id=0, has_side_effects=True),
-    )(tiles, meta, w_gate, w_up, w_down)
+    )(tokens, expert_ids, gate_probs, w_gate, w_up, w_down)
 
 
 def solution(mesh):

time: 112 us -> 106 us (0.946)
  Pallas kernels: 108 us -> 104 us
  other arithmetic: 1.53 us -> 0 us
    pallas_call x1, Pallas kernels: 108 us -> 104 us  [local(): pl.pallas_call(kernel, out_shape=jax.ShapeDtypeStruct((count, width), BF1...]
where the time goes in v2:
time: 106 us; the launch traced here: 105 us
  Pallas kernels  104 us (98%)
  local copies, waits for them, and re-layouts  1.39 us (1%)
    pallas_call x1, Pallas kernels, local(): pl.pallas_call(kernel, out_shape=jax.ShapeDtypeStruct((count, width), BF1...  104 us

profile of v2, /device:TPU:24, one launch (start us, length us, event | category | flops | bytes accessed | tf_op | source)
XLA Modules:
  0.0 105.4 jit_solution(4350192671632447956)
XLA Ops:
  0.0 104.1 %shard_map.64 = bf16[4,4096]{1,0:T(4,128)(2,1)} custom-call(bf16[4,4096]{1,0:T(4,128)(2,1)} %tokens.1, s32[4,8]{1,0:T(4,128)} %ids.1, f32[4,8]{1,0:T(4,128)} %gates.1, bf16[1,4096,128]{2,1,0:T(8,128)(2,1)} %wg.1, bf16[1,4096,128]{2,1,0:T(8,128)(2,1)} %wu.1, bf16[1,2048,256]{2,1,0:T(8,128)(2,1)} %wd.1), custom_call_target="tpu_custom_call" | custom-call | tf_op jit(solution)/shard_map/pallas_call | solution.py:355
  104.1 1.4 %copy.8 = bf16[4,4096]{1,0:T(4,128)(2,1)} copy(bf16[4,4096]{1,0:T(4,128)(2,1)} %shard_map.64) | data formatting | bytes 65536

commit v3 on v2

--- a/solution.py
+++ b/solution.py
@@ -252,9 +252,9 @@
             for step in (4, 3, 5, 2, 6, 1, 7):
                 hid_copy(n, step).start()
 
-        @pl.when(n >= 1)
+        @pl.when(n >= 3)
         def _():
-            b = n - 1
+            b = n - 3
             for step in range(1, NZ):
                 src = lax.rem(z + step, NZ)
                 pltpu.make_async_remote_copy(
@@ -279,7 +279,7 @@
 
         return carry
 
-    lax.fori_loop(0, 9, group, 0)
+    lax.fori_loop(0, 11, group, 0)
 
     def arrived(step, carry):
         src = lax.rem(ex + step, NE)

time: 106 us -> 105 us (level)
  the two profiles are of different devices: /device:TPU:24 before, /device:TPU:8 now
where the time goes in v3:
time: 105 us
  Pallas kernels  104 us (99%)
  local copies, waits for them, and re-layouts  1.39 us (1%)
    pallas_call x1, Pallas kernels, local(): pl.pallas_call(kernel, out_shape=jax.ShapeDtypeStruct((count, width), BF1...  104 us

profile of v3, /device:TPU:8, one launch (start us, length us, event | category | flops | bytes accessed | tf_op | source)
XLA Modules:
  0.0 105.1 jit_solution(1758187319777196777)
XLA Ops:
  0.0 103.7 %shard_map.64 = bf16[4,4096]{1,0:T(4,128)(2,1)} custom-call(bf16[4,4096]{1,0:T(4,128)(2,1)} %tokens.1, s32[4,8]{1,0:T(4,128)} %ids.1, f32[4,8]{1,0:T(4,128)} %gates.1, bf16[1,4096,128]{2,1,0:T(8,128)(2,1)} %wg.1, bf16[1,4096,128]{2,1,0:T(8,128)(2,1)} %wu.1, bf16[1,2048,256]{2,1,0:T(8,128)(2,1)} %wd.1), custom_call_target="tpu_custom_call" | custom-call | tf_op jit(solution)/shard_map/pallas_call | solution.py:355
  103.7 1.4 %copy.8 = bf16[4,4096]{1,0:T(4,128)(2,1)} copy(bf16[4,4096]{1,0:T(4,128)(2,1)} %shard_map.64) | data formatting | bytes 65536
